TPU v7x, 32 devices: a whole 2x2x4 slice. The times are simulated.
32 devices in a mesh: gz: 16 (over z, y, x), col: 2 (over core).
Axes of the slice: x: 2, y: 2, z: 4, core: 2. Of those that a mesh axis runs over, the one named last changes fastest.
Arguments:
- velocity: float32 [64, 3, 128, 128], P('gz', None, 'col'), may hold values from -6 to 6
- forces: float32 [3, 131072], P(None, ('gz', 'col')), may hold values from -60 to 60
- offsets: float32 [3, 131072], P(None, ('gz', 'col')), may hold values from 0 to 1
- cell_x: int32 [131072], P(('gz', 'col')), may hold values from 0 to 127
- cell_y: int32 [131072], P(('gz', 'col')), may hold values from 0 to 127
- cell_z: int32 [131072], P(('gz', 'col')), may hold values from 0 to 12
- band_start: int32 [16], P('gz'), may hold values from 0 to 15, as said below
Outputs:
- force_field: float32 [64, 3, 128, 128], P('gz', None, 'col')
- velocity_next: float32 [64, 3, 128, 128], P('gz', None, 'col')
Inputs may be any that keep to these rules, and one draw needn't show every extreme that they name: (g - band_start[g]) mod 16 lies in 0 to 3 for every gz index g.
All inputs are finite; a program needn't handle non-finite values.
Results may differ from a plain program's by a relative error of at most 0.0037.
Values sent between devices are 32-bit elements; how exact they have to be, the bound alone decides.
A program may use at most 64 MiB of HBM per device.

v0:
```python
import math

import jax
import jax.numpy as jnp
from jax import lax
from jax.sharding import PartitionSpec as P

BAND = 4


viscous = 0.15


def shifted(x, axis, by):
    devices = lax.axis_size(axis)
    return lax.ppermute(x, axis, [(i, (i + by) % devices) for i in range(devices)])


def extended(block, sides, width):
    for axis, dim in sides:
        count = lax.axis_size(axis)
        forward = [(i, i + 1) for i in range(count - 1)]
        forward.append((count - 1, 0))
        backward = [(target, source) for source, target in forward]
        low = lax.ppermute(
            lax.slice_in_dim(block, block.shape[dim] - width, None, axis=dim), axis, forward
        )
        high = lax.ppermute(lax.slice_in_dim(block, 0, width, axis=dim), axis, backward)
        block = jnp.concatenate([low, block, high], axis=dim)
    return block


def delta_weights(fraction):
    root_term = jnp.sqrt(1.0 + 4.0 * fraction - 4.0 * fraction * fraction)
    return jnp.stack(
        [
            (3.0 - 2.0 * fraction - root_term) / 8.0,
            (3.0 - 2.0 * fraction + root_term) / 8.0,
            (1.0 + 2.0 * fraction + root_term) / 8.0,
            (1.0 + 2.0 * fraction - root_term) / 8.0,
        ]
    )


def hit_matrix(points, weights, columns, period):
    result = jnp.zeros((points.shape[0], columns.shape[0]), jnp.float32)
    for corner in range(4):
        target = (points + corner) % period
        result = result + jnp.where(
            columns[None, :] == target[:, None], weights[corner][:, None], 0.0
        )
    return result


def spread_band(
    forces, offsets, cell_x, cell_y, cell_z, first_x, span_x, full_x, width_y, band_depth
):
    marker_count = cell_x.shape[0]
    block_size = math.gcd(marker_count, 256)
    turn_count = marker_count // block_size
    x_columns = first_x + jnp.arange(span_x, dtype=jnp.int32)
    y_columns = jnp.arange(width_y, dtype=jnp.int32)
    z_columns = jnp.arange(band_depth, dtype=jnp.int32)

    def one_block(totals, pieces):
        piece_x, piece_y, piece_z, piece_offsets, piece_forces = pieces
        x_weights = hit_matrix(piece_x, delta_weights(piece_offsets[0]), x_columns, full_x)
        y_weights = hit_matrix(piece_y, delta_weights(piece_offsets[1]), y_columns, width_y).astype(
            jnp.bfloat16
        )
        z_weights = hit_matrix(piece_z, delta_weights(piece_offsets[2]), z_columns, band_depth)
        scaled = (
            z_weights[:, :, None, None]
            * piece_forces.T[:, None, :, None]
            * x_weights[:, None, None, :]
        )
        scaled = scaled.reshape(block_size, band_depth * 3 * span_x).astype(jnp.bfloat16)
        product = lax.dot_general(
            scaled, y_weights, (((0,), (0,)), ((), ())), preferred_element_type=jnp.float32
        )
        return (totals + product, None)

    pieces = (
        cell_x.reshape(turn_count, block_size),
        cell_y.reshape(turn_count, block_size),
        cell_z.reshape(turn_count, block_size),
        offsets.reshape(3, turn_count, block_size).transpose(1, 0, 2),
        forces.reshape(3, turn_count, block_size).transpose(1, 0, 2),
    )
    totals = jnp.zeros((band_depth * 3 * span_x, width_y), jnp.float32)
    totals = lax.scan(one_block, totals, pieces)[0]
    return totals.reshape(band_depth, 3, span_x, width_y)


def on_device(velocity, forces, offsets, cell_x, cell_y, cell_z, band_start):
    slab_depth, components, half_x, width_y = velocity.shape
    gz_count = lax.axis_size("gz")
    gz_index = lax.axis_index("gz")
    col_index = lax.axis_index("col")
    full_x = half_x * lax.axis_size("col")
    band_depth = BAND * slab_depth
    cell_x, cell_y, cell_z, offsets, forces = (
        lax.all_gather(cell_x, "col", axis=0, tiled=True),
        lax.all_gather(cell_y, "col", axis=0, tiled=True),
        lax.all_gather(cell_z, "col", axis=0, tiled=True),
        lax.all_gather(offsets, "col", axis=1, tiled=True),
        lax.all_gather(forces, "col", axis=1, tiled=True),
    )
    band_field = spread_band(
        forces,
        offsets,
        cell_x,
        cell_y,
        cell_z,
        col_index * half_x,
        half_x,
        full_x,
        width_y,
        band_depth,
    )
    behind = (gz_index - band_start[0]) % gz_count
    window = jnp.zeros(((2 * BAND - 1) * slab_depth, components, half_x, width_y), jnp.float32)
    window = lax.dynamic_update_slice_in_dim(
        window, band_field, (BAND - 1 - behind) * slab_depth, 0
    )
    center = window[(BAND - 1) * slab_depth : BAND * slab_depth]
    upper_part = window[(BAND - 1) * slab_depth :]
    lower_part = (
        window[: BAND * slab_depth]
        .reshape(BAND, slab_depth, components, half_x, width_y)[::-1]
        .reshape(BAND * slab_depth, components, half_x, width_y)
    )
    stride = BAND // 2
    while stride >= 1:
        upper_part = upper_part[: stride * slab_depth] + shifted(
            upper_part[stride * slab_depth :], "gz", stride
        )
        lower_part = lower_part[: stride * slab_depth] + shifted(
            lower_part[stride * slab_depth :], "gz", -stride
        )
        stride = stride // 2
    own_slabs = upper_part + lower_part - center
    padded = extended(velocity, (("gz", 0), ("col", 2)), 1)
    neighbours = padded[2:, :, 1:-1] + padded[:-2, :, 1:-1]
    neighbours = neighbours + padded[1:-1, :, 2:] + padded[1:-1, :, :-2]
    neighbours = neighbours + jnp.roll(velocity, 1, 3) + jnp.roll(velocity, -1, 3)
    velocity_next = velocity + viscous * (neighbours - 6.0 * velocity) + own_slabs
    return (own_slabs, velocity_next)


def solution(mesh):
    in_specs = (
        P("gz", None, "col", None),
        P(None, ("gz", "col")),
        P(None, ("gz", "col")),
        P(("gz", "col")),
        P(("gz", "col")),
        P(("gz", "col")),
        P("gz"),
    )
    out_specs = (P("gz", None, "col", None), P("gz", None, "col", None))
    return jax.shard_map(
        on_device, mesh=mesh, in_specs=in_specs, out_specs=out_specs, check_vma=False
    )
```

profile of v0, /device:TPU:5, one launch (start us, length us, event | category | flops | bytes accessed | tf_op | source)
XLA Modules:
  0.0 148.8 jit_solution(4947236822957068371)
XLA Ops:
  1.3 2.4 %all_gather.16 = f32[3,8192]{1,0:T(4,128)S(1)} all-gather(f32[3,4096]{1,0:T(4,128)} %param.11), channel_id=1, replica_groups=mesh['gz'=16,'col'=2] {'col'}, dimensions={1}, use_global_device_ids=true | all-gather | bytes 147456 | tf_op jit(solution)/shard_map/all_gather | solution.py:106
  3.7 2.1 %all_gather.17 = f32[3,8192]{1,0:T(4,128)S(1)} all-gather(f32[3,4096]{1,0:T(4,128)} %param.10), channel_id=1, replica_groups=mesh['gz'=16,'col'=2] {'col'}, dimensions={1}, use_global_device_ids=true | all-gather | bytes 147456 | tf_op jit(solution)/shard_map/all_gather | solution.py:107
  5.8 2.0 %all_gather.15 = s32[8192]{0:T(1024)S(1)} all-gather(s32[4096]{0:T(1024)} %param.14), channel_id=1, replica_groups=mesh['gz'=16,'col'=2] {'col'}, dimensions={0}, use_global_device_ids=true | all-gather | bytes 49152 | tf_op jit(solution)/shard_map/all_gather | solution.py:105
  7.9 2.0 %all_gather.18 = s32[8192]{0:T(1024)S(1)} all-gather(s32[4096]{0:T(1024)} %param.12), channel_id=1, replica_groups=mesh['gz'=16,'col'=2] {'col'}, dimensions={0}, use_global_device_ids=true | all-gather | bytes 49152 | tf_op jit(solution)/shard_map/all_gather | solution.py:103
  10.0 2.0 %all_gather.19 = s32[8192]{0:T(1024)S(1)} all-gather(s32[4096]{0:T(1024)} %param.13), channel_id=1, replica_groups=mesh['gz'=16,'col'=2] {'col'}, dimensions={0}, use_global_device_ids=true | all-gather | bytes 49152 | tf_op jit(solution)/shard_map/all_gather | solution.py:104
  12.0 61.3 %while.15 = (s32[]{:T(128)}, f32[3072,128]{1,0:T(8,128)S(1)}, s32[32,256]{1,0:T(8,128)S(1)}, f32[32,3,256]{2,1,0:T(4,128)S(1)}, f32[32,3,256]{2,1,0:T(4,128)S(1)...) while((s32[]{:T(128)}, f32[3072,128]{1,0:T(8,128)S(1)}, ...), condition=%wide.region_1.2_spmd.clone.clone, body=%wide.region_0.1_spmd.clone.clone.sunk | while | flops 204364352 | bytes 6631091 | solution.py:91
  12.9 1.0 convolution_add_fusion.2
  20.6 1.0 convolution_add_fusion.2
  24.4 1.0 convolution_add_fusion.2
  28.2 1.0 convolution_add_fusion.2
  32.0 1.0 convolution_add_fusion.2
  35.9 1.0 convolution_add_fusion.2
  39.7 1.0 convolution_add_fusion.2
  73.9 1.3 collective-permute-start
  75.2 17.5 %collective-permute-done = f32[8,3,64,128]{3,2,1,0:T(8,128)S(1)} collective-permute-done((f32[8,3,64,128]{3,2,1,0:T(8,128)S(1)}, f32[8,3,64,128]{3,2,1,0:T(8,128)S(1)}, u32[]{:S(2)}, u32[]{:S(2)}) %collective-permute-start) | collective-permute-done | bytes 786464 | tf_op jit(solution)/shard_map/ppermute | solution.py:16
  93.9 3.3 %collective-permute-start.2 = (f32[8,3,64,128]{3,2,1,0:T(8,128)}, f32[8,3,64,128]{3,2,1,0:T(8,128)}, u32[]{:S(2)}, u32[]{:S(2)}) collective-permute-start(f32[8,3,64,128]{3,2,1,0:T(8,128)} %bitcast.9), channel_id=1, source_target_pairs={{0,28},{2,30},{4,0},{6,2},{8,4},{10,6},{12,8},{14,10},{16,12},{18,... | collective-permute-start | bytes 2359304 | tf_op jit(solution)/shard_map/ppermute | solution.py:16
  97.2 1.1 collective-permute-start.5
  98.3 1.3 collective-permute-start.4
  99.8 2.9 %collective-permute-done.5 = f32[1,3,64,128]{3,2,1,0:T(8,128)S(1)} collective-permute-done((f32[1,3,64,128]{3,2,1,0:T(8,128)S(1)}, f32[1,3,64,128]{3,2,1,0:T(8,128)S(1)}, u32[]{:S(2)}, u32[]{:S(2)}) %collective-permute-start.5) | collective-permute-done | bytes 98336 | tf_op jit(solution)/shard_map/ppermute | solution.py:25
  103.7 21.9 %collective-permute-start.1 = (f32[4,3,64,128]{3,2,1,0:T(8,128)S(1)}, f32[4,3,64,128]{3,2,1,0:T(8,128)S(1)}, u32[]{:S(2)}, u32[]{:S(2)}) collective-permute-start(f32[4,3,64,128]{3,2,1,0:T(8,128)S(1)} %slice.155), channel_id=1, source_target_pairs={{0,2},{2,4},{4,6},{6,8},{8,10},{10,12},{12,14},{14,16},{16,18},{18... | collective-permute-start | bytes 1179656 | tf_op jit(solution)/shard_map/ppermute | solution.py:16
  125.6 1.2 bitcast_add_fusion
  127.0 3.4 %collective-permute-start.6 = (f32[6,3,1,128]{3,2,1,0:T(1,128)S(1)}, f32[6,3,1,128]{3,2,1,0:T(1,128)S(1)}, u32[]{:S(2)}, u32[]{:S(2)}) collective-permute-start(f32[6,3,1,128]{3,2,1,0:T(1,128)S(1)} %get-tuple-element.293), channel_id=1, source_target_pairs={{1,0},{0,1},{3,2},{2,3},{5,4},{4,5},{7,6},{6,7},{9,8},{8,9},{11,10... | collective-permute-start | bytes 27656 | tf_op jit(solution)/shard_map/ppermute | solution.py:28
  131.5 14.8 %collective-permute-done.3 = f32[4,3,64,128]{3,2,1,0:T(8,128)S(1)} collective-permute-done((f32[4,3,64,128]{3,2,1,0:T(8,128)S(1)}, f32[4,3,64,128]{3,2,1,0:T(8,128)S(1)}, u32[]{:S(2)}, u32[]{:S(2)}) %collective-permute-start.3) | collective-permute-done | bytes 393248 | tf_op jit(solution)/shard_map/ppermute | solution.py:16
  146.4 2.4 %fusion.40 = (f32[4,3,64,128]{3,2,1,0:T(8,128)}, f32[4,3,64,128]{3,2,1,0:T(8,128)}) fusion(f32[4,3,64,128]{3,2,1,0:T(8,128)S(1)} %copy-done, f32[6,3,64,128]{3,2,1,0:T(8,128)S(1)} %copy-done.3, f32[6,3,1,128]{3,2,1,0:T(1,128)S(1)} %collective-permute-done.7, f32[6,3,1,128]{3,2,1,0:T(1,128)S(1)} %collective-permute-done.6, ...), kind=kLoop, calls=%fused_computation.119 | loop fusion | flops 1966080 | bytes 4737024 | tf_op jit(solution)/shard_map/add | solution.py:147
  (547 shorter events, 54.1 us)
Async XLA Ops:
  73.8 19.1 %copy-start.1 = (f32[28,3,64,128]{3,2,1,0:T(8,128)}, f32[28,3,64,128]{3,2,1,0:T(8,128)S(1)}, u32[]{:S(2)}) copy-start(f32[28,3,64,128]{3,2,1,0:T(8,128)S(1)} %constant_dynamic-update-slice_fusion.3) | copy-start | bytes 8257540
  73.9 18.8 %collective-permute-start = (f32[8,3,64,128]{3,2,1,0:T(8,128)S(1)}, f32[8,3,64,128]{3,2,1,0:T(8,128)S(1)}, u32[]{:S(2)}, u32[]{:S(2)}) collective-permute-start(f32[8,3,64,128]{3,2,1,0:T(8,128)S(1)} %slice.153), channel_id=1, source_target_pairs={{0,4},{2,6},{4,8},{6,10},{8,12},{10,14},{12,16},{14,18},{16,20},{1... | collective-permute-start | bytes 2359304 | tf_op jit(solution)/shard_map/ppermute | solution.py:16
  93.0 4.3 %copy-start = (f32[4,3,64,128]{3,2,1,0:T(8,128)S(1)}, f32[4,3,64,128]{3,2,1,0:T(8,128)}, u32[]{:S(2)}) copy-start(f32[4,3,64,128]{3,2,1,0:T(8,128)} %param.9) | copy-start | bytes 1179652
  93.9 31.7 %collective-permute-start.2 = (f32[8,3,64,128]{3,2,1,0:T(8,128)}, f32[8,3,64,128]{3,2,1,0:T(8,128)}, u32[]{:S(2)}, u32[]{:S(2)}) collective-permute-start(f32[8,3,64,128]{3,2,1,0:T(8,128)} %bitcast.9), channel_id=1, source_target_pairs={{0,28},{2,30},{4,0},{6,2},{8,4},{10,6},{12,8},{14,10},{16,12},{18,... | collective-permute-start | bytes 2359304 | tf_op jit(solution)/shard_map/ppermute | solution.py:16
  97.2 5.5 %collective-permute-start.5 = (f32[1,3,64,128]{3,2,1,0:T(8,128)S(1)}, f32[1,3,64,128]{3,2,1,0:T(8,128)S(1)}, u32[]{:S(2)}, u32[]{:S(2)}) collective-permute-start(f32[1,3,64,128]{3,2,1,0:T(8,128)S(1)} %get-tuple-element.300), channel_id=1, source_target_pairs={{0,2},{2,4},{4,6},{6,8},{8,10},{10,12},{12,14},{14,16},{16,18},{18... | collective-permute-start | bytes 294920 | tf_op jit(solution)/shard_map/ppermute | solution.py:25
  98.3 4.4 %collective-permute-start.4 = (f32[1,3,64,128]{3,2,1,0:T(8,128)S(1)}, f32[1,3,64,128]{3,2,1,0:T(8,128)S(1)}, u32[]{:S(2)}, u32[]{:S(2)}) collective-permute-start(f32[1,3,64,128]{3,2,1,0:T(8,128)S(1)} %get-tuple-element.299), channel_id=1, source_target_pairs={{2,0},{4,2},{6,4},{8,6},{10,8},{12,10},{14,12},{16,14},{18,16},{20... | collective-permute-start | bytes 294920 | tf_op jit(solution)/shard_map/ppermute | solution.py:28
  102.7 0.6 copy-start.4
  102.8 0.6 copy-start.6
  102.8 0.8 copy-start.2
  103.7 23.2 %copy-start.3 = (f32[6,3,64,128]{3,2,1,0:T(8,128)S(1)}, f32[6,3,64,128]{3,2,1,0:T(8,128)}, u32[]{:S(2)}) copy-start(f32[6,3,64,128]{3,2,1,0:T(8,128)} %copy-done.2) | copy-start | bytes 1769476
  103.7 27.8 %collective-permute-start.1 = (f32[4,3,64,128]{3,2,1,0:T(8,128)S(1)}, f32[4,3,64,128]{3,2,1,0:T(8,128)S(1)}, u32[]{:S(2)}, u32[]{:S(2)}) collective-permute-start(f32[4,3,64,128]{3,2,1,0:T(8,128)S(1)} %slice.155), channel_id=1, source_target_pairs={{0,2},{2,4},{4,6},{6,8},{8,10},{10,12},{12,14},{14,16},{16,18},{18... | collective-permute-start | bytes 1179656 | tf_op jit(solution)/shard_map/ppermute | solution.py:16
  126.8 19.5 %copy-start.5 = (f32[1,3,64,128]{3,2,1,0:T(8,128)S(1)}, f32[1,3,64,128]{3,2,1,0:T(8,128)}, u32[]{:S(2)}) copy-start(f32[1,3,64,128]{3,2,1,0:T(8,128)} %copy-done.4) | copy-start | bytes 294916
  126.8 19.5 %copy-start.7 = (f32[1,3,64,128]{3,2,1,0:T(8,128)S(1)}, f32[1,3,64,128]{3,2,1,0:T(8,128)}, u32[]{:S(2)}) copy-start(f32[1,3,64,128]{3,2,1,0:T(8,128)} %copy-done.6) | copy-start | bytes 294916
  126.9 19.5 %collective-permute-start.3 = (f32[4,3,64,128]{3,2,1,0:T(8,128)S(1)}, f32[4,3,64,128]{3,2,1,0:T(8,128)S(1)}, u32[]{:S(2)}, u32[]{:S(2)}) collective-permute-start(f32[4,3,64,128]{3,2,1,0:T(8,128)S(1)} %slice.159), channel_id=1, source_target_pairs={{0,30},{2,0},{4,2},{6,4},{8,6},{10,8},{12,10},{14,12},{16,14},{18,... | collective-permute-start | bytes 1179656 | tf_op jit(solution)/shard_map/ppermute | solution.py:16
  127.0 4.2 %collective-permute-start.6 = (f32[6,3,1,128]{3,2,1,0:T(1,128)S(1)}, f32[6,3,1,128]{3,2,1,0:T(1,128)S(1)}, u32[]{:S(2)}, u32[]{:S(2)}) collective-permute-start(f32[6,3,1,128]{3,2,1,0:T(1,128)S(1)} %get-tuple-element.293), channel_id=1, source_target_pairs={{1,0},{0,1},{3,2},{2,3},{5,4},{4,5},{7,6},{6,7},{9,8},{8,9},{11,10... | collective-permute-start | bytes 27656 | tf_op jit(solution)/shard_map/ppermute | solution.py:28
  130.4 1.2 collective-permute-start.7
where the time goes:
time: 149 us
  waiting for transfers between devices  36.1 us (24%)
  matrix products  33.2 us (22%)
  starting transfers between devices  32.4 us (22%)
  other arithmetic  26.3 us (18%)
  blocking collectives  10.7 us (7%)
  local copies, waits for them, and re-layouts  4.41 us (3%)
  loops' own time  4.07 us (3%)
  between operations  1.54 us (1%)
    dot_general x32, matrix products, one_block(): lax.dot_general(scaled, y_weights, (((0,), (0,)), ((), ())), preferred_el...  33.2 us
    ppermute x4, waiting for transfers between devices, shifted(): lax.ppermute(x, axis, [(i, (i + by) % devices) for i in range(devices)])  32.3 us
    ppermute x4, starting transfers between devices, shifted(): lax.ppermute(x, axis, [(i, (i + by) % devices) for i in range(devices)])  26.5 us
    convert_element_type x32, other arithmetic, one_block(): scaled.reshape(block_size, band_depth * 3 * span_x).astype(jnp.bfloat16)  16 us
    ppermute x2, starting transfers between devices, extended(): lax.ppermute(lax.slice_in_dim(block, 0, width, axis=dim), axis, backward)  4.68 us
    another operation x1, loops' own time, spread_band(): totals = lax.scan(one_block, totals, pieces)[0]  4.07 us
    add x64, other arithmetic, hit_matrix(): result + jnp.where(columns[None, :] == target[:, None], weights[corner][:...  3.52 us
    ppermute x2, waiting for transfers between devices, extended(): lax.ppermute(lax.slice_in_dim(block, block.shape[dim] - width, None, axis...  3.22 us
  transfers between devices with their start and end apart: 8, of which 5 were waited for; matrix products, arithmetic and copies ran while one was open for 1% of the time, Pallas kernels for 0%

commit v1 on v0

v1 whole, which is shorter than its diff:
```python
import functools

import jax
import jax.numpy as jnp
from jax import lax
from jax.experimental import pallas as pl
from jax.experimental.pallas import tpu as pltpu
from jax.sharding import PartitionSpec as P

BAND = 4
CORNERS = 4
VISCOUS = 0.15
LANES = 128
SUBLANES = 8
GROUPS = 4
MESH = pl.DeviceIdType.MESH


def delta_weights(fraction):
    root_term = jnp.sqrt(1.0 + 4.0 * fraction - 4.0 * fraction * fraction)
    return (
        (3.0 - 2.0 * fraction - root_term) / 8.0,
        (3.0 - 2.0 * fraction + root_term) / 8.0,
        (1.0 + 2.0 * fraction + root_term) / 8.0,
        (1.0 + 2.0 * fraction - root_term) / 8.0,
    )


def pick(distance, weights):
    result = jnp.where(distance == 0, weights[0], 0.0)
    for corner in range(1, CORNERS):
        result = jnp.where(distance == corner, weights[corner], result)
    return result


def wrapped(distance, period):
    if period & (period - 1) == 0:
        return distance & (period - 1)
    return jnp.where(distance < 0, distance + period, distance)


def kernel(
    sizes,
    packed_ref,
    velocity_ref,
    field_ref,
    next_ref,
    markers,
    left,
    right,
    total,
    outgoing,
    incoming,
    z_halo,
    x_halo,
    send_sems,
    recv_sems,
):
    gz_count, col_count, slab_depth, half_x, width_y, rows_each = sizes
    full_x = half_x * col_count
    full_z = slab_depth * gz_count
    group_x = full_x // GROUPS
    local_x = group_x + SUBLANES
    gz = lax.axis_index("gz")
    col = lax.axis_index("col")
    steps = [by for reach in range(1, BAND) for by in (reach, -reach)]

    def gz_at(by):
        return lax.rem(gz + (by + gz_count), gz_count)

    other_col = lax.rem(col + 1, col_count)

    barrier = pltpu.get_barrier_semaphore()
    for by in steps:
        pl.semaphore_signal(barrier, inc=1, device_id={"gz": gz_at(by)}, device_id_type=MESH)
    pl.semaphore_signal(barrier, inc=1, device_id={"col": other_col}, device_id_type=MESH)
    pl.semaphore_wait(barrier, len(steps) + 1)

    copies = []

    def send(source, target, slot, device):
        copy = pltpu.make_async_remote_copy(
            src_ref=source,
            dst_ref=target,
            send_sem=send_sems.at[slot],
            recv_sem=recv_sems.at[slot],
            device_id=device,
            device_id_type=MESH,
        )
        copy.start()
        copies.append(copy)
        return copy

    for slot, by in enumerate(steps):
        send(packed_ref, markers.at[slot + 1], slot + 1, {"gz": gz_at(by)})
    base = len(steps) + 1
    halos = [
        send(velocity_ref.at[slab_depth - 1], z_halo.at[0], base, {"gz": gz_at(1)}),
        send(velocity_ref.at[0], z_halo.at[1], base + 1, {"gz": gz_at(-1)}),
        send(
            velocity_ref.at[:, :, half_x - SUBLANES : half_x],
            x_halo.at[0],
            base + 2,
            {"col": other_col},
        ),
        send(velocity_ref.at[:, :, 0:SUBLANES], x_halo.at[1], base + 3, {"col": other_col}),
    ]

    markers[0] = packed_ref[...]
    total[...] = jnp.zeros_like(total)

    first_x = col * half_x
    first_z = gz * slab_depth
    pieces = rows_each // SUBLANES
    y_rows = lax.broadcasted_iota(jnp.int32, (width_y, LANES), 0)
    x_rows = lax.broadcasted_iota(jnp.int32, (local_x, LANES), 0)

    def fill(source, piece):
        start = pl.multiple_of(piece * SUBLANES, SUBLANES)

        def param(index):
            return markers[source, pl.ds(index * rows_each + start, SUBLANES), :]

        forces = [param(c) for c in range(3)]
        wx = delta_weights(param(3))
        wy = delta_weights(param(4))
        wz = delta_weights(param(5))
        x_rel = wrapped(param(6).astype(jnp.int32) - first_x, full_x)
        y_cell = param(7).astype(jnp.int32)
        z_cell = param(8).astype(jnp.int32)
        group = x_rel // group_x
        x_local = x_rel - group * group_x
        members = [jnp.where(group == g, 1.0, 0.0) for g in range(GROUPS)]
        scaled = []
        for plane in range(slab_depth):
            z_weight = pick(wrapped(plane + first_z - z_cell, full_z), wz)
            scaled.extend(z_weight * force for force in forces)
        for row in range(SUBLANES):
            lanes = slice(row * LANES, (row + 1) * LANES)

            def line(value):
                return value[row : row + 1, :]

            y_hits = pick(
                wrapped(y_rows - line(y_cell), width_y), [line(w) for w in wy]
            ).astype(jnp.bfloat16)
            for g in range(GROUPS):
                member = jnp.broadcast_to(line(members[g]), (width_y, LANES)).astype(jnp.bfloat16)
                right[g * width_y : (g + 1) * width_y, lanes] = y_hits * member
            x_hits = pick(x_rows - line(x_local), [line(w) for w in wx])
            for pair in range(len(scaled) // 2):
                both = jnp.concatenate(
                    [line(scaled[2 * pair]) * x_hits, line(scaled[2 * pair + 1]) * x_hits], axis=0
                )
                left[2 * pair * local_x : 2 * (pair + 1) * local_x, lanes] = both.astype(jnp.bfloat16)

    def one_source(source, _):
        @pl.when(source > 0)
        def _():
            pltpu.make_async_remote_copy(
                src_ref=packed_ref,
                dst_ref=markers.at[source],
                send_sem=send_sems.at[source],
                recv_sem=recv_sems.at[source],
                device_id={"gz": gz_at(1)},
                device_id_type=MESH,
            ).wait_recv()

        def one_piece(piece, _):
            fill(source, piece)
            total[...] += lax.dot_general(
                left[...],
                right[...],
                (((1,), (1,)), ((), ())),
                preferred_element_type=jnp.float32,
            )
            return 0

        lax.fori_loop(0, pieces, one_piece, 0)
        return 0

    lax.fori_loop(0, len(steps) + 1, one_source, 0)

    own_groups = GROUPS // col_count

    def gathered(plane, component, group):
        start = (plane * 3 + component) * local_x
        main = total[start : start + group_x, group * width_y : (group + 1) * width_y]
        before = (group - 1) % GROUPS
        spill = total[
            start + group_x : start + local_x, before * width_y : (before + 1) * width_y
        ]
        return main, spill

    def put(target, plane, component, group, place):
        main, spill = gathered(plane, component, group)
        start = place * group_x
        target[plane, component, start : start + SUBLANES, :] = main[:SUBLANES] + spill
        target[plane, component, start + SUBLANES : start + group_x, :] = main[SUBLANES:]

    for plane in range(slab_depth):
        for component in range(3):
            for place in range(own_groups):
                put(outgoing, plane, component, own_groups + place, place)
    exchange = send(outgoing, incoming, base + 4, {"col": other_col})

    for halo in halos:
        halo.wait_recv()
    x_index = lax.broadcasted_iota(jnp.int32, (half_x, width_y), 0)
    for plane in range(slab_depth):
        for component in range(3):
            for place in range(own_groups):
                put(field_ref, plane, component, place, place)
            here = velocity_ref[plane, component]
            below = z_halo[0, component] if plane == 0 else velocity_ref[plane - 1, component]
            above = (
                z_halo[1, component]
                if plane == slab_depth - 1
                else velocity_ref[plane + 1, component]
            )
            low = x_halo[0, plane, component, SUBLANES - 1 : SUBLANES, :]
            high = x_halo[1, plane, component, 0:1, :]
            x_low = jnp.where(x_index == 0, low, pltpu.roll(here, 1, 0))
            x_high = jnp.where(x_index == half_x - 1, high, pltpu.roll(here, half_x - 1, 0))
            near = above + below + x_low + x_high
            near = near + pltpu.roll(here, 1, 1) + pltpu.roll(here, width_y - 1, 1)
            next_ref[plane, component] = here + VISCOUS * (near - 6.0 * here)

    exchange.wait_recv()
    for plane in range(slab_depth):
        for component in range(3):
            own = field_ref[plane, component] + incoming[plane, component]
            field_ref[plane, component] = own
            next_ref[plane, component] = next_ref[plane, component] + own
    for copy in copies:
        copy.wait_send()


def on_device(sizes, velocity, forces, offsets, cell_x, cell_y, cell_z, band_start):
    gz_count, col_count, slab_depth, half_x, width_y, rows_each = sizes
    full_x = half_x * col_count
    full_z = slab_depth * gz_count
    z_cell = (band_start[0] * slab_depth + cell_z) % full_z
    cells = jnp.stack([cell_x, cell_y, z_cell]).astype(jnp.float32)
    packed = jnp.concatenate([forces, offsets, cells], axis=0).reshape(9 * rows_each, LANES)
    sources = 2 * BAND - 1
    local_x = full_x // GROUPS + SUBLANES
    left_rows = slab_depth * 3 * local_x
    right_rows = GROUPS * width_y
    block = SUBLANES * LANES
    shape = jax.ShapeDtypeStruct(velocity.shape, jnp.float32)
    copies = sources + 5
    return pl.pallas_call(
        functools.partial(kernel, sizes),
        out_shape=(shape, shape),
        in_specs=[pl.BlockSpec(memory_space=pltpu.VMEM)] * 2,
        out_specs=(pl.BlockSpec(memory_space=pltpu.VMEM),) * 2,
        scratch_shapes=[
            pltpu.VMEM((sources, 9 * rows_each, LANES), jnp.float32),
            pltpu.VMEM((left_rows, block), jnp.bfloat16),
            pltpu.VMEM((right_rows, block), jnp.bfloat16),
            pltpu.VMEM((left_rows, right_rows), jnp.float32),
            pltpu.VMEM(velocity.shape, jnp.float32),
            pltpu.VMEM(velocity.shape, jnp.float32),
            pltpu.VMEM((2,) + velocity.shape[1:], jnp.float32),
            pltpu.VMEM((2, slab_depth, 3, SUBLANES, width_y), jnp.float32),
            pltpu.SemaphoreType.DMA((copies,)),
            pltpu.SemaphoreType.DMA((copies,)),
        ],
        compiler_params=pltpu.CompilerParams(
            collective_id=0, has_side_effects=True, vmem_limit_bytes=48 * 1024 * 1024
        ),
    )(packed, velocity)


def solution(mesh):
    from_shapes = functools.partial(sized, mesh)
    in_specs = (
        P("gz", None, "col", None),
        P(None, ("gz", "col")),
        P(None, ("gz", "col")),
        P(("gz", "col")),
        P(("gz", "col")),
        P(("gz", "col")),
        P("gz"),
    )
    out_specs = (P("gz", None, "col", None), P("gz", None, "col", None))
    return jax.shard_map(
        from_shapes, mesh=mesh, in_specs=in_specs, out_specs=out_specs, check_vma=False
    )


def sized(mesh, velocity, forces, offsets, cell_x, cell_y, cell_z, band_start):
    slab_depth, _, half_x, width_y = velocity.shape
    rows_each = cell_x.shape[0] // LANES
    sizes = (mesh.shape["gz"], mesh.shape["col"], slab_depth, half_x, width_y, rows_each)
    return on_device(sizes, velocity, forces, offsets, cell_x, cell_y, cell_z, band_start)
```

time: 149 us -> 50.4 us (0.34)
  the two profiles are of different devices: /device:TPU:5 before, /device:TPU:27 now
where the time goes in v1:
time: 50.4 us; the launch traced here: 50 us
  Pallas kernels  44.6 us (88%)
  local copies, waits for them, and re-layouts  2.44 us (5%)
  other arithmetic  1.62 us (3%)
  between operations  1.35 us (3%)
    pallas_call x1, Pallas kernels, on_device(): pl.pallas_call(functools.partial(kernel, sizes), out_shape=(shape, shape)...  44.6 us
    unnamed x10, local copies, waits for them, and re-layouts  2.41 us

profile of v1, /device:TPU:27, one launch (start us, length us, event | category | flops | bytes accessed | tf_op | source)
XLA Modules:
  0.0 50.0 jit_solution(554838789564963604)
XLA Ops:
  1.3 0.0 copy-start.3
  1.3 0.0 copy-start.2
  1.3 0.8 %add_select_fusion = s32[4096]{0:T(1024)S(1)} fusion(s32[4096]{0:T(1024)} %param.12, s32[]{:T(128)} %bitcast.2), kind=kLoop, calls=%fused_computation.2 | loop fusion | flops 49152 | bytes 32772 | tf_op jit(solution)/shard_map/jit(remainder)/select_n | solution.py:243
  2.1 0.0 copy-start.1
  2.1 0.0 copy-done.3
  2.1 0.8 %add_convert_fusion = f32[3,4096]{1,0:T(4,128)S(1)} fusion(s32[1,4096]{1,0:T(1,128)S(1)} %bitcast.4, s32[1,4096]{1,0:T(1,128)S(1)} %bitcast.5, s32[1,4096]{1,0:T(1,128)} %bitcast.6), kind=kLoop, calls=%fused_computation.1 | loop fusion | flops 36864 | bytes 98304 | tf_op jit(solution)/shard_map/convert_element_type | solution.py:244
  2.9 0.0 copy-done.2
  2.9 0.0 copy-done.1
  2.9 0.0 copy-start
  2.9 0.1 pad_maximum_fusion
  3.0 0.9 %copy-done = f32[4,3,64,128]{3,2,1,0:T(8,128)S(1)} copy-done((f32[4,3,64,128]{3,2,1,0:T(8,128)S(1)}, f32[4,3,64,128]{3,2,1,0:T(8,128)}, u32[]{:S(2)}) %copy-start) | copy-done | bytes 393240
  3.9 44.6 %shard_map.86 = (f32[4,3,64,128]{3,2,1,0:T(8,128)S(1)}, f32[4,3,64,128]{3,2,1,0:T(8,128)S(1)}) custom-call(f32[288,128]{1,0:T(8,128)S(1)} %reshape.9.packed_ref, f32[4,3,64,128]{3,2,1,0:T(8,128)S(1)} %copy-done), custom_call_target="tpu_custom_call" | custom-call | tf_op jit(solution)/shard_map/pallas_call | solution.py:253
  48.5 0.7 %copy.12 = f32[4,3,64,128]{3,2,1,0:T(8,128)} copy(f32[4,3,64,128]{3,2,1,0:T(8,128)S(1)} %get-tuple-element.4) | data formatting | bytes 786432
  49.2 0.7 %copy.13 = f32[4,3,64,128]{3,2,1,0:T(8,128)} copy(f32[4,3,64,128]{3,2,1,0:T(8,128)S(1)} %get-tuple-element.5) | data formatting | bytes 786432
  (1 shorter events, 0.0 us)
Async XLA Ops:
  1.3 0.8 %copy-start.3 = (s32[4096]{0:T(1024)S(1)}, s32[4096]{0:T(1024)}, u32[]{:S(2)}) copy-start(s32[4096]{0:T(1024)} %param.11) | copy-start | bytes 49156
  1.3 1.6 %copy-start.2 = (f32[3,4096]{1,0:T(4,128)S(1)}, f32[3,4096]{1,0:T(4,128)}, u32[]{:S(2)}) copy-start(f32[3,4096]{1,0:T(4,128)} %param.8) | copy-start | bytes 147460
  2.1 0.8 %copy-start.1 = (f32[3,4096]{1,0:T(4,128)S(1)}, f32[3,4096]{1,0:T(4,128)}, u32[]{:S(2)}) copy-start(f32[3,4096]{1,0:T(4,128)} %param.9) | copy-start | bytes 147460
  2.9 1.0 %copy-start = (f32[4,3,64,128]{3,2,1,0:T(8,128)S(1)}, f32[4,3,64,128]{3,2,1,0:T(8,128)}, u32[]{:S(2)}) copy-start(f32[4,3,64,128]{3,2,1,0:T(8,128)} %velocity_ref.1) | copy-start | bytes 1179652

commit v2 on v1

--- a/solution.py
+++ b/solution.py
@@ -12,6 +12,7 @@
 VISCOUS = 0.15
 LANES = 128
 SUBLANES = 8
+PIECE_ROWS = 32
 GROUPS = 4
 MESH = pl.DeviceIdType.MESH
 
@@ -111,22 +112,31 @@
 
     first_x = col * half_x
     first_z = gz * slab_depth
-    pieces = rows_each // SUBLANES
-    y_rows = lax.broadcasted_iota(jnp.int32, (width_y, LANES), 0)
+    pieces = rows_each // PIECE_ROWS
+    y_rows = [
+        (lax.broadcasted_iota(jnp.int32, (2 * SUBLANES, LANES), 0) + start)
+        .astype(jnp.float32)
+        .astype(jnp.bfloat16)
+        for start in range(0, width_y, 2 * SUBLANES)
+    ]
     x_rows = lax.broadcasted_iota(jnp.int32, (local_x, LANES), 0)
 
     def fill(source, piece):
-        start = pl.multiple_of(piece * SUBLANES, SUBLANES)
+        start = pl.multiple_of(piece * PIECE_ROWS, SUBLANES)
 
         def param(index):
-            return markers[source, pl.ds(index * rows_each + start, SUBLANES), :]
+            return markers[source, pl.ds(index * rows_each + start, PIECE_ROWS), :]
 
         forces = [param(c) for c in range(3)]
         wx = delta_weights(param(3))
         wy = delta_weights(param(4))
         wz = delta_weights(param(5))
         x_rel = wrapped(param(6).astype(jnp.int32) - first_x, full_x)
-        y_cell = param(7).astype(jnp.int32)
+        y_cell = param(7)
+        targets = []
+        for corner in range(CORNERS):
+            target = y_cell + corner
+            targets.append(jnp.where(target >= width_y, target - width_y, target))
         z_cell = param(8).astype(jnp.int32)
         group = x_rel // group_x
         x_local = x_rel - group * group_x
@@ -135,24 +145,33 @@
         for plane in range(slab_depth):
             z_weight = pick(wrapped(plane + first_z - z_cell, full_z), wz)
             scaled.extend(z_weight * force for force in forces)
-        for row in range(SUBLANES):
+        for row in range(PIECE_ROWS):
             lanes = slice(row * LANES, (row + 1) * LANES)
 
             def line(value):
                 return value[row : row + 1, :]
 
-            y_hits = pick(
-                wrapped(y_rows - line(y_cell), width_y), [line(w) for w in wy]
-            ).astype(jnp.bfloat16)
-            for g in range(GROUPS):
-                member = jnp.broadcast_to(line(members[g]), (width_y, LANES)).astype(jnp.bfloat16)
-                right[g * width_y : (g + 1) * width_y, lanes] = y_hits * member
+            def packed_line(value):
+                wide = jnp.broadcast_to(line(value), (2 * SUBLANES, LANES))
+                return wide.astype(jnp.bfloat16)
+
+            y_targets = [packed_line(target) for target in targets]
+            y_weights = [packed_line(w) for w in wy]
+            y_members = [packed_line(member) for member in members]
+            for part in range(width_y // (2 * SUBLANES)):
+                y_row = y_rows[part]
+                hits = jnp.zeros((2 * SUBLANES, LANES), jnp.bfloat16)
+                for target, weight in zip(y_targets, y_weights):
+                    hits = jnp.where(y_row == target, weight, hits)
+                for g in range(GROUPS):
+                    start_row = g * width_y + part * 2 * SUBLANES
+                    right[start_row : start_row + 2 * SUBLANES, lanes] = (hits * y_members[g]).astype(jnp.float32)
             x_hits = pick(x_rows - line(x_local), [line(w) for w in wx])
             for pair in range(len(scaled) // 2):
                 both = jnp.concatenate(
                     [line(scaled[2 * pair]) * x_hits, line(scaled[2 * pair + 1]) * x_hits], axis=0
                 )
-                left[2 * pair * local_x : 2 * (pair + 1) * local_x, lanes] = both.astype(jnp.bfloat16)
+                left[2 * pair * local_x : 2 * (pair + 1) * local_x, lanes] = both
 
     def one_source(source, _):
         @pl.when(source > 0)
@@ -247,7 +266,7 @@
     local_x = full_x // GROUPS + SUBLANES
     left_rows = slab_depth * 3 * local_x
     right_rows = GROUPS * width_y
-    block = SUBLANES * LANES
+    block = PIECE_ROWS * LANES
     shape = jax.ShapeDtypeStruct(velocity.shape, jnp.float32)
     copies = sources + 5
     return pl.pallas_call(
@@ -257,8 +276,8 @@
         out_specs=(pl.BlockSpec(memory_space=pltpu.VMEM),) * 2,
         scratch_shapes=[
             pltpu.VMEM((sources, 9 * rows_each, LANES), jnp.float32),
-            pltpu.VMEM((left_rows, block), jnp.bfloat16),
-            pltpu.VMEM((right_rows, block), jnp.bfloat16),
+            pltpu.VMEM((left_rows, block), jnp.float32),
+            pltpu.VMEM((right_rows, block), jnp.float32),
             pltpu.VMEM((left_rows, right_rows), jnp.float32),
             pltpu.VMEM(velocity.shape, jnp.float32),
             pltpu.VMEM(velocity.shape, jnp.float32),

time: 50.4 us -> 40.5 us (0.80)
  the two profiles are of different devices: /device:TPU:27 before, /device:TPU:0 now
where the time goes in v2:
time: 40.5 us; the launch traced here: 40.1 us
  Pallas kernels  34.7 us (86%)
  local copies, waits for them, and re-layouts  2.44 us (6%)
  other arithmetic  1.62 us (4%)
  between operations  1.35 us (3%)
    pallas_call x1, Pallas kernels, on_device(): pl.pallas_call(functools.partial(kernel, sizes), out_shape=(shape, shape)...  34.7 us
    unnamed x10, local copies, waits for them, and re-layouts  2.41 us

profile of v2, /device:TPU:0, one launch (start us, length us, event | category | flops | bytes accessed | tf_op | source)
XLA Modules:
  0.0 40.1 jit_solution(17443474276409837064)
XLA Ops:
  1.3 0.0 copy-start.3
  1.3 0.0 copy-start.2
  1.3 0.8 %add_select_fusion = s32[4096]{0:T(1024)S(1)} fusion(s32[4096]{0:T(1024)} %param.12, s32[]{:T(128)} %bitcast.2), kind=kLoop, calls=%fused_computation.2 | loop fusion | flops 49152 | bytes 32772 | tf_op jit(solution)/shard_map/jit(remainder)/select_n | solution.py:262
  2.1 0.0 copy-start.1
  2.1 0.0 copy-done.3
  2.1 0.8 %add_convert_fusion = f32[3,4096]{1,0:T(4,128)S(1)} fusion(s32[1,4096]{1,0:T(1,128)S(1)} %bitcast.4, s32[1,4096]{1,0:T(1,128)S(1)} %bitcast.5, s32[1,4096]{1,0:T(1,128)} %bitcast.6), kind=kLoop, calls=%fused_computation.1 | loop fusion | flops 36864 | bytes 98304 | tf_op jit(solution)/shard_map/convert_element_type | solution.py:263
  2.9 0.0 copy-done.2
  2.9 0.0 copy-done.1
  2.9 0.0 copy-start
  2.9 0.1 pad_maximum_fusion
  3.0 0.9 %copy-done = f32[4,3,64,128]{3,2,1,0:T(8,128)S(1)} copy-done((f32[4,3,64,128]{3,2,1,0:T(8,128)S(1)}, f32[4,3,64,128]{3,2,1,0:T(8,128)}, u32[]{:S(2)}) %copy-start) | copy-done | bytes 393240
  3.9 34.7 %shard_map.86 = (f32[4,3,64,128]{3,2,1,0:T(8,128)S(1)}, f32[4,3,64,128]{3,2,1,0:T(8,128)S(1)}) custom-call(f32[288,128]{1,0:T(8,128)S(1)} %reshape.9.packed_ref, f32[4,3,64,128]{3,2,1,0:T(8,128)S(1)} %copy-done), custom_call_target="tpu_custom_call" | custom-call | tf_op jit(solution)/shard_map/pallas_call | solution.py:272
  38.6 0.7 %copy.12 = f32[4,3,64,128]{3,2,1,0:T(8,128)} copy(f32[4,3,64,128]{3,2,1,0:T(8,128)S(1)} %get-tuple-element.4) | data formatting | bytes 786432
  39.4 0.7 %copy.13 = f32[4,3,64,128]{3,2,1,0:T(8,128)} copy(f32[4,3,64,128]{3,2,1,0:T(8,128)S(1)} %get-tuple-element.5) | data formatting | bytes 786432
  (1 shorter events, 0.0 us)
Async XLA Ops:
  1.3 0.8 %copy-start.3 = (s32[4096]{0:T(1024)S(1)}, s32[4096]{0:T(1024)}, u32[]{:S(2)}) copy-start(s32[4096]{0:T(1024)} %param.11) | copy-start | bytes 49156
  1.3 1.6 %copy-start.2 = (f32[3,4096]{1,0:T(4,128)S(1)}, f32[3,4096]{1,0:T(4,128)}, u32[]{:S(2)}) copy-start(f32[3,4096]{1,0:T(4,128)} %param.8) | copy-start | bytes 147460
  2.1 0.8 %copy-start.1 = (f32[3,4096]{1,0:T(4,128)S(1)}, f32[3,4096]{1,0:T(4,128)}, u32[]{:S(2)}) copy-start(f32[3,4096]{1,0:T(4,128)} %param.9) | copy-start | bytes 147460
  2.9 1.0 %copy-start = (f32[4,3,64,128]{3,2,1,0:T(8,128)S(1)}, f32[4,3,64,128]{3,2,1,0:T(8,128)}, u32[]{:S(2)}) copy-start(f32[4,3,64,128]{3,2,1,0:T(8,128)} %velocity_ref.1) | copy-start | bytes 1179652

commit v3 on v2

--- a/solution.py
+++ b/solution.py
@@ -64,7 +64,13 @@
     local_x = group_x + SUBLANES
     gz = lax.axis_index("gz")
     col = lax.axis_index("col")
-    steps = [by for reach in range(1, BAND) for by in (reach, -reach)]
+    place_in_band = lax.rem(gz, BAND)
+    low_bit, high_bit = lax.rem(place_in_band, 2), place_in_band // 2
+    near = [1 - 2 * low_bit, 2 - 4 * high_bit, 3 - 2 * place_in_band]
+    far = [by - BAND + 2 * BAND * bit for by, bit in zip(near, (low_bit, high_bit, high_bit))]
+    steps = [near[0], near[1], near[2], far[1], far[0], far[2]]
+    starts = [0, 0, 1, 2, 2, 3]
+    halo_start = 4
 
     def gz_at(by):
         return lax.rem(gz + (by + gz_count), gz_count)
@@ -77,10 +83,10 @@
     pl.semaphore_signal(barrier, inc=1, device_id={"col": other_col}, device_id_type=MESH)
     pl.semaphore_wait(barrier, len(steps) + 1)
 
-    copies = []
-
-    def send(source, target, slot, device):
-        copy = pltpu.make_async_remote_copy(
+    base = len(steps) + 1
+
+    def remote(source, target, slot, device):
+        return pltpu.make_async_remote_copy(
             src_ref=source,
             dst_ref=target,
             send_sem=send_sems.at[slot],
@@ -88,24 +94,26 @@
             device_id=device,
             device_id_type=MESH,
         )
-        copy.start()
-        copies.append(copy)
-        return copy
-
-    for slot, by in enumerate(steps):
-        send(packed_ref, markers.at[slot + 1], slot + 1, {"gz": gz_at(by)})
-    base = len(steps) + 1
+
+    travels = [
+        remote(packed_ref, markers.at[slot + 1], slot + 1, {"gz": gz_at(by)})
+        for slot, by in enumerate(steps)
+    ]
     halos = [
-        send(velocity_ref.at[slab_depth - 1], z_halo.at[0], base, {"gz": gz_at(1)}),
-        send(velocity_ref.at[0], z_halo.at[1], base + 1, {"gz": gz_at(-1)}),
-        send(
+        remote(velocity_ref.at[slab_depth - 1], z_halo.at[0], base, {"gz": gz_at(1)}),
+        remote(velocity_ref.at[0], z_halo.at[1], base + 1, {"gz": gz_at(-1)}),
+        remote(
             velocity_ref.at[:, :, half_x - SUBLANES : half_x],
             x_halo.at[0],
             base + 2,
             {"col": other_col},
         ),
-        send(velocity_ref.at[:, :, 0:SUBLANES], x_halo.at[1], base + 3, {"col": other_col}),
+        remote(velocity_ref.at[:, :, 0:SUBLANES], x_halo.at[1], base + 3, {"col": other_col}),
     ]
+    exchange = remote(outgoing, incoming, base + 4, {"col": other_col})
+    for travel, start in zip(travels, starts):
+        if start == 0:
+            travel.start()
 
     markers[0] = packed_ref[...]
     total[...] = jnp.zeros_like(total)
@@ -174,16 +182,22 @@
                 left[2 * pair * local_x : 2 * (pair + 1) * local_x, lanes] = both
 
     def one_source(source, _):
+        for begin in sorted(set(starts) - {0}):
+
+            @pl.when(source == begin)
+            def _():
+                for travel, start in zip(travels, starts):
+                    if start == begin:
+                        travel.start()
+
+        @pl.when(source == halo_start)
+        def _():
+            for halo in halos:
+                halo.start()
+
         @pl.when(source > 0)
         def _():
-            pltpu.make_async_remote_copy(
-                src_ref=packed_ref,
-                dst_ref=markers.at[source],
-                send_sem=send_sems.at[source],
-                recv_sem=recv_sems.at[source],
-                device_id={"gz": gz_at(1)},
-                device_id_type=MESH,
-            ).wait_recv()
+            remote(packed_ref, markers.at[source], source, {"gz": gz_at(1)}).wait_recv()
 
         def one_piece(piece, _):
             fill(source, piece)
@@ -221,7 +235,7 @@
         for component in range(3):
             for place in range(own_groups):
                 put(outgoing, plane, component, own_groups + place, place)
-    exchange = send(outgoing, incoming, base + 4, {"col": other_col})
+    exchange.start()
 
     for halo in halos:
         halo.wait_recv()
@@ -241,9 +255,9 @@
             high = x_halo[1, plane, component, 0:1, :]
             x_low = jnp.where(x_index == 0, low, pltpu.roll(here, 1, 0))
             x_high = jnp.where(x_index == half_x - 1, high, pltpu.roll(here, half_x - 1, 0))
-            near = above + below + x_low + x_high
-            near = near + pltpu.roll(here, 1, 1) + pltpu.roll(here, width_y - 1, 1)
-            next_ref[plane, component] = here + VISCOUS * (near - 6.0 * here)
+            around = above + below + x_low + x_high
+            around = around + pltpu.roll(here, 1, 1) + pltpu.roll(here, width_y - 1, 1)
+            next_ref[plane, component] = here + VISCOUS * (around - 6.0 * here)
 
     exchange.wait_recv()
     for plane in range(slab_depth):
@@ -251,7 +265,7 @@
             own = field_ref[plane, component] + incoming[plane, component]
             field_ref[plane, component] = own
             next_ref[plane, component] = next_ref[plane, component] + own
-    for copy in copies:
+    for copy in travels + halos + [exchange]:
         copy.wait_send()
 
 

time: 40.5 us -> 34.9 us (0.86)
  Pallas kernels: 34.7 us -> 29.1 us
    pallas_call x1, Pallas kernels: 34.7 us -> 29.1 us  [on_device(): pl.pallas_call(functools.partial(kernel, sizes), out_shape=(shape, shape)...]
where the time goes in v3:
time: 34.9 us; the launch traced here: 34.5 us
  Pallas kernels  29.1 us (83%)
  local copies, waits for them, and re-layouts  2.44 us (7%)
  other arithmetic  1.62 us (5%)
  between operations  1.35 us (4%)
    pallas_call x1, Pallas kernels, on_device(): pl.pallas_call(functools.partial(kernel, sizes), out_shape=(shape, shape)...  29.1 us
    unnamed x10, local copies, waits for them, and re-layouts  2.41 us
    convert_element_type x1, other arithmetic, on_device(): cells = jnp.stack([cell_x, cell_y, z_cell]).astype(jnp.float32)  0.8 us
    select_n x1, other arithmetic, on_device(): z_cell = (band_start[0] * slab_depth + cell_z) % full_z  0.76 us

profile of v3, /device:TPU:0, one launch (start us, length us, event | category | flops | bytes accessed | tf_op | source)
XLA Modules:
  0.0 34.5 jit_solution(15141753307047232199)
XLA Ops:
  1.3 0.0 copy-start.3
  1.3 0.0 copy-start.2
  1.3 0.8 %add_select_fusion = s32[4096]{0:T(1024)S(1)} fusion(s32[4096]{0:T(1024)} %param.12, s32[]{:T(128)} %bitcast.2), kind=kLoop, calls=%fused_computation.2 | loop fusion | flops 49152 | bytes 32772 | tf_op jit(solution)/shard_map/jit(remainder)/select_n | solution.py:276
  2.1 0.0 copy-start.1
  2.1 0.0 copy-done.3
  2.1 0.8 %add_convert_fusion = f32[3,4096]{1,0:T(4,128)S(1)} fusion(s32[1,4096]{1,0:T(1,128)S(1)} %bitcast.4, s32[1,4096]{1,0:T(1,128)S(1)} %bitcast.5, s32[1,4096]{1,0:T(1,128)} %bitcast.6), kind=kLoop, calls=%fused_computation.1 | loop fusion | flops 36864 | bytes 98304 | tf_op jit(solution)/shard_map/convert_element_type | solution.py:277
  2.9 0.0 copy-done.2
  2.9 0.0 copy-done.1
  2.9 0.0 copy-start
  2.9 0.1 pad_maximum_fusion
  3.0 0.9 %copy-done = f32[4,3,64,128]{3,2,1,0:T(8,128)S(1)} copy-done((f32[4,3,64,128]{3,2,1,0:T(8,128)S(1)}, f32[4,3,64,128]{3,2,1,0:T(8,128)}, u32[]{:S(2)}) %copy-start) | copy-done | bytes 393240
  3.9 29.1 %shard_map.86 = (f32[4,3,64,128]{3,2,1,0:T(8,128)S(1)}, f32[4,3,64,128]{3,2,1,0:T(8,128)S(1)}) custom-call(f32[288,128]{1,0:T(8,128)S(1)} %reshape.9.packed_ref, f32[4,3,64,128]{3,2,1,0:T(8,128)S(1)} %copy-done), custom_call_target="tpu_custom_call" | custom-call | tf_op jit(solution)/shard_map/pallas_call | solution.py:286
  33.0 0.7 %copy.12 = f32[4,3,64,128]{3,2,1,0:T(8,128)} copy(f32[4,3,64,128]{3,2,1,0:T(8,128)S(1)} %get-tuple-element.4) | data formatting | bytes 786432
  33.8 0.7 %copy.13 = f32[4,3,64,128]{3,2,1,0:T(8,128)} copy(f32[4,3,64,128]{3,2,1,0:T(8,128)S(1)} %get-tuple-element.5) | data formatting | bytes 786432
  (1 shorter events, 0.0 us)
Async XLA Ops:
  1.3 0.8 %copy-start.3 = (s32[4096]{0:T(1024)S(1)}, s32[4096]{0:T(1024)}, u32[]{:S(2)}) copy-start(s32[4096]{0:T(1024)} %param.11) | copy-start | bytes 49156
  1.3 1.6 %copy-start.2 = (f32[3,4096]{1,0:T(4,128)S(1)}, f32[3,4096]{1,0:T(4,128)}, u32[]{:S(2)}) copy-start(f32[3,4096]{1,0:T(4,128)} %param.8) | copy-start | bytes 147460
  2.1 0.8 %copy-start.1 = (f32[3,4096]{1,0:T(4,128)S(1)}, f32[3,4096]{1,0:T(4,128)}, u32[]{:S(2)}) copy-start(f32[3,4096]{1,0:T(4,128)} %param.9) | copy-start | bytes 147460
  2.9 1.0 %copy-start = (f32[4,3,64,128]{3,2,1,0:T(8,128)S(1)}, f32[4,3,64,128]{3,2,1,0:T(8,128)}, u32[]{:S(2)}) copy-start(f32[4,3,64,128]{3,2,1,0:T(8,128)} %velocity_ref.1) | copy-start | bytes 1179652

commit v4 on v3

--- a/solution.py
+++ b/solution.py
@@ -43,7 +43,7 @@
 def kernel(
     sizes,
     packed_ref,
-    velocity_ref,
+    velocity_hbm,
     field_ref,
     next_ref,
     markers,
@@ -54,6 +54,8 @@
     incoming,
     z_halo,
     x_halo,
+    velocity_ref,
+    load_sem,
     send_sems,
     recv_sems,
 ):
@@ -61,7 +63,7 @@
     full_x = half_x * col_count
     full_z = slab_depth * gz_count
     group_x = full_x // GROUPS
-    local_x = group_x + SUBLANES
+    main_rows = slab_depth * 3 * group_x
     gz = lax.axis_index("gz")
     col = lax.axis_index("col")
     place_in_band = lax.rem(gz, BAND)
@@ -115,6 +117,8 @@
         if start == 0:
             travel.start()
 
+    load = pltpu.make_async_copy(velocity_hbm, velocity_ref, load_sem)
+    load.start()
     markers[0] = packed_ref[...]
     total[...] = jnp.zeros_like(total)
 
@@ -127,7 +131,10 @@
         .astype(jnp.bfloat16)
         for start in range(0, width_y, 2 * SUBLANES)
     ]
-    x_rows = lax.broadcasted_iota(jnp.int32, (local_x, LANES), 0)
+    x_rows = lax.broadcasted_iota(jnp.int32, (group_x, LANES), 0)
+    eight = lax.broadcasted_iota(jnp.int32, (SUBLANES, LANES), 0)
+    first_half = eight < CORNERS
+    spill_rows = group_x + jnp.where(first_half, eight, eight - CORNERS)
 
     def fill(source, piece):
         start = pl.multiple_of(piece * PIECE_ROWS, SUBLANES)
@@ -174,12 +181,15 @@
                 for g in range(GROUPS):
                     start_row = g * width_y + part * 2 * SUBLANES
                     right[start_row : start_row + 2 * SUBLANES, lanes] = (hits * y_members[g]).astype(jnp.float32)
-            x_hits = pick(x_rows - line(x_local), [line(w) for w in wx])
+            x_weights = [line(w) for w in wx]
+            x_hits = pick(x_rows - line(x_local), x_weights)
+            spill_hits = pick(spill_rows - line(x_local), x_weights)
+            for index, value in enumerate(scaled):
+                left[index * group_x : (index + 1) * group_x, lanes] = line(value) * x_hits
             for pair in range(len(scaled) // 2):
-                both = jnp.concatenate(
-                    [line(scaled[2 * pair]) * x_hits, line(scaled[2 * pair + 1]) * x_hits], axis=0
-                )
-                left[2 * pair * local_x : 2 * (pair + 1) * local_x, lanes] = both
+                both = jnp.where(first_half, line(scaled[2 * pair]), line(scaled[2 * pair + 1]))
+                start_row = main_rows + pair * SUBLANES
+                left[start_row : start_row + SUBLANES, lanes] = both * spill_hits
 
     def one_source(source, _):
         for begin in sorted(set(starts) - {0}):
@@ -192,6 +202,7 @@
 
         @pl.when(source == halo_start)
         def _():
+            load.wait()
             for halo in halos:
                 halo.start()
 
@@ -216,13 +227,18 @@
 
     own_groups = GROUPS // col_count
 
+    spill_keep = lax.broadcasted_iota(jnp.int32, (SUBLANES, width_y), 0) < CORNERS
+
     def gathered(plane, component, group):
-        start = (plane * 3 + component) * local_x
+        index = plane * 3 + component
+        start = index * group_x
         main = total[start : start + group_x, group * width_y : (group + 1) * width_y]
         before = (group - 1) % GROUPS
-        spill = total[
-            start + group_x : start + local_x, before * width_y : (before + 1) * width_y
-        ]
+        start = main_rows + index // 2 * SUBLANES
+        spill = total[start : start + SUBLANES, before * width_y : (before + 1) * width_y]
+        if index % 2 == 1:
+            spill = pltpu.roll(spill, CORNERS, 0)
+        spill = jnp.where(spill_keep, spill, 0.0)
         return main, spill
 
     def put(target, plane, component, group, place):
@@ -277,8 +293,8 @@
     cells = jnp.stack([cell_x, cell_y, z_cell]).astype(jnp.float32)
     packed = jnp.concatenate([forces, offsets, cells], axis=0).reshape(9 * rows_each, LANES)
     sources = 2 * BAND - 1
-    local_x = full_x // GROUPS + SUBLANES
-    left_rows = slab_depth * 3 * local_x
+    group_x = full_x // GROUPS
+    left_rows = slab_depth * 3 * group_x + (slab_depth * 3 + 1) // 2 * SUBLANES
     right_rows = GROUPS * width_y
     block = PIECE_ROWS * LANES
     shape = jax.ShapeDtypeStruct(velocity.shape, jnp.float32)
@@ -286,7 +302,7 @@
     return pl.pallas_call(
         functools.partial(kernel, sizes),
         out_shape=(shape, shape),
-        in_specs=[pl.BlockSpec(memory_space=pltpu.VMEM)] * 2,
+        in_specs=[pl.BlockSpec(memory_space=pltpu.VMEM), pl.BlockSpec(memory_space=pl.ANY)],
         out_specs=(pl.BlockSpec(memory_space=pltpu.VMEM),) * 2,
         scratch_shapes=[
             pltpu.VMEM((sources, 9 * rows_each, LANES), jnp.float32),
@@ -297,6 +313,8 @@
             pltpu.VMEM(velocity.shape, jnp.float32),
             pltpu.VMEM((2,) + velocity.shape[1:], jnp.float32),
             pltpu.VMEM((2, slab_depth, 3, SUBLANES, width_y), jnp.float32),
+            pltpu.VMEM(velocity.shape, jnp.float32),
+            pltpu.SemaphoreType.DMA,
             pltpu.SemaphoreType.DMA((copies,)),
             pltpu.SemaphoreType.DMA((copies,)),
         ],

time: 34.9 us -> 34.8 us (level)
  Pallas kernels: 29.1 us -> 28.7 us
    pallas_call x1, Pallas kernels: 29.1 us -> 28.7 us  [on_device(): pl.pallas_call(functools.partial(kernel, sizes), out_shape=(shape, shape)...]
where the time goes in v4:
time: 34.8 us; the launch traced here: 34.1 us
  Pallas kernels  28.7 us (82%)
  local copies, waits for them, and re-layouts  2.44 us (7%)
  other arithmetic  1.62 us (5%)
  between operations  1.35 us (4%)
    pallas_call x1, Pallas kernels, on_device(): pl.pallas_call(functools.partial(kernel, sizes), out_shape=(shape, shape)...  28.7 us
    unnamed x10, local copies, waits for them, and re-layouts  2.41 us
    convert_element_type x1, other arithmetic, on_device(): cells = jnp.stack([cell_x, cell_y, z_cell]).astype(jnp.float32)  0.8 us
    select_n x1, other arithmetic, on_device(): z_cell = (band_start[0] * slab_depth + cell_z) % full_z  0.76 us

profile of v4, /device:TPU:0, one launch (start us, length us, event | category | flops | bytes accessed | tf_op | source)
XLA Modules:
  0.0 34.1 jit_solution(5136996429725963912)
XLA Ops:
  1.3 0.0 copy-start.3
  1.3 0.0 copy-start.2
  1.3 0.8 %add_select_fusion = s32[4096]{0:T(1024)S(1)} fusion(s32[4096]{0:T(1024)} %param.12, s32[]{:T(128)} %bitcast.2), kind=kLoop, calls=%fused_computation.2 | loop fusion | flops 49152 | bytes 32772 | tf_op jit(solution)/shard_map/jit(remainder)/select_n | solution.py:292
  2.1 0.0 copy-start.1
  2.1 0.0 copy-done.3
  2.1 0.8 %add_convert_fusion = f32[3,4096]{1,0:T(4,128)S(1)} fusion(s32[1,4096]{1,0:T(1,128)S(1)} %bitcast.4, s32[1,4096]{1,0:T(1,128)S(1)} %bitcast.5, s32[1,4096]{1,0:T(1,128)} %bitcast.6), kind=kLoop, calls=%fused_computation.1 | loop fusion | flops 36864 | bytes 98304 | tf_op jit(solution)/shard_map/convert_element_type | solution.py:293
  2.9 0.0 copy-done.2
  2.9 0.0 copy-done.1
  2.9 0.0 copy-start
  2.9 0.1 pad_maximum_fusion
  3.0 0.9 %copy-done = f32[4,3,64,128]{3,2,1,0:T(8,128)S(1)} copy-done((f32[4,3,64,128]{3,2,1,0:T(8,128)S(1)}, f32[4,3,64,128]{3,2,1,0:T(8,128)}, u32[]{:S(2)}) %copy-start) | copy-done | bytes 393240
  3.9 28.7 %shard_map.86 = (f32[4,3,64,128]{3,2,1,0:T(8,128)S(1)}, f32[4,3,64,128]{3,2,1,0:T(8,128)S(1)}) custom-call(f32[288,128]{1,0:T(8,128)S(1)} %reshape.9.packed_ref, f32[4,3,64,128]{3,2,1,0:T(8,128)S(1)} %copy-done), custom_call_target="tpu_custom_call" | custom-call | tf_op jit(solution)/shard_map/pallas_call | solution.py:302
  32.6 0.7 %copy.12 = f32[4,3,64,128]{3,2,1,0:T(8,128)} copy(f32[4,3,64,128]{3,2,1,0:T(8,128)S(1)} %get-tuple-element.4) | data formatting | bytes 786432
  33.4 0.7 %copy.13 = f32[4,3,64,128]{3,2,1,0:T(8,128)} copy(f32[4,3,64,128]{3,2,1,0:T(8,128)S(1)} %get-tuple-element.5) | data formatting | bytes 786432
  (1 shorter events, 0.0 us)
Async XLA Ops:
  1.3 0.8 %copy-start.3 = (s32[4096]{0:T(1024)S(1)}, s32[4096]{0:T(1024)}, u32[]{:S(2)}) copy-start(s32[4096]{0:T(1024)} %param.11) | copy-start | bytes 49156
  1.3 1.6 %copy-start.2 = (f32[3,4096]{1,0:T(4,128)S(1)}, f32[3,4096]{1,0:T(4,128)}, u32[]{:S(2)}) copy-start(f32[3,4096]{1,0:T(4,128)} %param.8) | copy-start | bytes 147460
  2.1 0.8 %copy-start.1 = (f32[3,4096]{1,0:T(4,128)S(1)}, f32[3,4096]{1,0:T(4,128)}, u32[]{:S(2)}) copy-start(f32[3,4096]{1,0:T(4,128)} %param.9) | copy-start | bytes 147460
  2.9 1.0 %copy-start = (f32[4,3,64,128]{3,2,1,0:T(8,128)S(1)}, f32[4,3,64,128]{3,2,1,0:T(8,128)}, u32[]{:S(2)}) copy-start(f32[4,3,64,128]{3,2,1,0:T(8,128)} %velocity_hbm.1) | copy-start | bytes 1179652
